TPU v7x, 32 devices: a whole 2x2x4 slice. The times are simulated.
32 devices in a mesh: dp: 16 (over z, y, core), tensor: 2 (over x).
Axes of the slice: x: 2, y: 2, z: 4, core: 2. Of those that a mesh axis runs over, the one named last changes fastest.
Arguments:
- patches: bfloat16 [37632, 768], P(('dp', 'tensor')), may hold values from -6 to 6
- gain_first: bfloat16 [768], replicated, may hold values from 0.099609375 to 1.8984375
- shift_first: bfloat16 [768], replicated, may hold values from -3 to 3
- attend_weight: bfloat16 [768, 2304], P(None, 'tensor'), may hold values from -0.21875 to 0.21875
- attend_bias: bfloat16 [24, 2, 32], P('tensor'), may hold values from -3 to 3
- offset_table: bfloat16 [24, 169], P('tensor'), may hold values from -5 to 5
- output_weight: bfloat16 [768, 768], P('tensor'), may hold values from -0.625 to 0.625
- output_bias: bfloat16 [768], replicated, may hold values from -3 to 3
- gain_second: bfloat16 [768], replicated, may hold values from 0.099609375 to 1.8984375
- shift_second: bfloat16 [768], replicated, may hold values from -3 to 3
- expand_weight: bfloat16 [768, 3072], P(None, 'tensor'), may hold values from -0.21875 to 0.21875
- expand_bias: bfloat16 [3072], P('tensor'), may hold values from -3 to 3
- reduce_weight: bfloat16 [3072, 768], P('tensor'), may hold values from -0.109375 to 0.109375
- reduce_bias: bfloat16 [768], replicated, may hold values from -3 to 3
- crop_counts: int32 [96], P('dp'), may hold values from 2 to 10, as said below
- cotangent: bfloat16 [37632, 768], P(('dp', 'tensor')), may hold values from -6 to 6
Outputs:
- result: bfloat16 [37632, 768], P(('dp', 'tensor'))
- input_grad: float32 [37632, 768], P(('dp', 'tensor'))
- gain_first_grad: float32 [768], P('tensor')
- shift_first_grad: float32 [768], P('tensor')
- attend_weight_grad: float32 [768, 2304], P(None, 'tensor')
- attend_bias_grad: float32 [24, 2, 32], P('tensor')
- offset_table_grad: float32 [24, 169], P('tensor')
- output_weight_grad: float32 [768, 768], P('tensor')
- output_bias_grad: float32 [768], P('tensor')
- gain_second_grad: float32 [768], P('tensor')
- shift_second_grad: float32 [768], P('tensor')
- expand_weight_grad: float32 [768, 3072], P(None, 'tensor')
- expand_bias_grad: float32 [3072], P('tensor')
- reduce_weight_grad: float32 [3072, 768], P('tensor')
- reduce_bias_grad: float32 [768], P('tensor')
Inputs may be any that keep to these rules, and one draw needn't show every extreme that they name: `crop_counts`: in each index of dp the counts of its 6 images sum to exactly 36, so their 2 + count windows fill its 48 window slots in order.
All inputs are finite; a program needn't handle non-finite values.
Results may differ from a plain program's by a relative error of at most 0.02.
Values may be sent and summed in bfloat16 or wider, within the bound.
No kernel may reach another device: no remote copies, remote signals or barrier semaphores. Data moves between devices by JAX's collectives and lax.ppermute only.
A program may use at most 256 MiB of HBM per device.

v0:
```python
from functools import partial
import jax
import jax.numpy as jnp
from jax import lax
from jax.sharding import PartitionSpec as P

HEAD_DIM = 32
HIGH = lax.Precision.HIGHEST
EPSILON = 1e-05
MASKED = 30000.0
SIDE = 7


def window_live(counts, slots):
    totals = counts + 2
    ends = jnp.cumsum(totals, dtype=jnp.int32)
    starts = ends - totals
    places = jnp.arange(slots, dtype=jnp.int32)[:, None]
    inside = (places >= starts[None, :]) & (places < ends[None, :])
    offset = jnp.sum(jnp.where(inside, places - starts[None, :], 0), axis=1, dtype=jnp.int32)
    present = jnp.any(inside, axis=1)
    spots = jnp.arange(SIDE * SIDE, dtype=jnp.int32)
    corner = (spots // SIDE < 3) & (spots % SIDE < 3)
    whole = present & (offset < 2)
    partial_win = present & (offset >= 2)
    alive = whole[:, None] | partial_win[:, None] & corner[None, :]
    return alive.astype(jnp.float32)


def offset_selector():
    spots = jnp.arange(SIDE * SIDE, dtype=jnp.int32)
    row_of = spots // SIDE
    col_of = spots % SIDE
    index = (
        (row_of[:, None] - row_of[None, :] + SIDE - 1) * (2 * SIDE - 1)
        + col_of[:, None]
        - col_of[None, :]
        + SIDE
        - 1
    )
    codes = jnp.arange((2 * SIDE - 1) ** 2, dtype=jnp.int32)
    return (codes[:, None] == index.reshape(1, -1)).astype(jnp.float32)


def norm_rows(values, gain, shift):
    mean = jnp.mean(values, axis=1, keepdims=True)
    centred = values - mean
    scale = lax.rsqrt(jnp.mean(centred * centred, axis=1, keepdims=True) + EPSILON)
    normal = centred * scale
    return (normal * gain + shift, normal, scale)


def norm_back(grad, normal, scale, gain):
    gain_grad = jnp.sum(grad * normal, axis=0)
    shift_grad = jnp.sum(grad, axis=0)
    inner = grad * gain
    centred = inner - jnp.mean(inner, axis=1, keepdims=True)
    return (
        scale * (centred - normal * jnp.mean(inner * normal, axis=1, keepdims=True)),
        gain_grad,
        shift_grad,
    )


def tdot(left, right):
    return lax.dot_general(
        left, right, (((0,), (0,)), ((), ())), preferred_element_type=jnp.float32
    )


def rdot(left, right):
    return lax.dot_general(
        left, right, (((1,), (1,)), ((), ())), preferred_element_type=jnp.float32
    )


def split_parts(block):
    query = (block[..., 0, :] * HEAD_DIM ** (-0.5)).astype(jnp.bfloat16)
    return (query, block[..., 1, :].astype(jnp.bfloat16), block[..., 2, :].astype(jnp.bfloat16))


def score_block(query, key, relative, mask):
    scores = jnp.einsum("wihd,wjhd->whij", query, key, preferred_element_type=jnp.float32)
    return scores + relative[None] + mask[:, None, None, :]


def block_layout(alive):
    windows = alive.shape[0]
    group = 8 if windows % 8 == 0 else windows
    return (windows, group, windows // group)


def attend_forward(packed, relative, alive, heads):
    windows, group, blocks = block_layout(alive)
    slots = SIDE * SIDE
    tiles = packed.reshape(blocks, group, slots, heads, 3, HEAD_DIM)
    masks = ((alive - 1.0) * MASKED).reshape(blocks, group, slots)

    def one(args):
        tile, mask = args
        query, key, value = split_parts(tile)
        scores = score_block(query, key, relative, mask)
        peak = jnp.max(scores, axis=3, keepdims=True)
        expo = jnp.exp(scores - peak)
        total = jnp.sum(expo, axis=3, keepdims=True)
        probs = (expo / total).astype(jnp.bfloat16)
        mixed = jnp.einsum("whij,wjhd->wihd", probs, value, preferred_element_type=jnp.float32)
        return (
            mixed.astype(jnp.bfloat16).reshape(group * slots, heads * HEAD_DIM),
            (peak + jnp.log(total))[..., 0],
        )

    mixed, norms = lax.map(one, (tiles, masks))
    return (mixed.reshape(windows * slots, heads * HEAD_DIM), norms)


def attend_backward(packed, mixed_grad, norms, relative, alive, heads):
    windows, group, blocks = block_layout(alive)
    slots = SIDE * SIDE
    tiles = packed.reshape(blocks, group, slots, heads, 3, HEAD_DIM)
    grads = mixed_grad.reshape(blocks, group, slots, heads, HEAD_DIM)
    masks = ((alive - 1.0) * MASKED).reshape(blocks, group, slots)

    def one(carry, args):
        tile, grad, mask, norm = args
        query, key, value = split_parts(tile)
        scores = score_block(query, key, relative, mask)
        soft = jnp.exp(scores - norm[..., None])
        probs = soft.astype(jnp.bfloat16)
        prob_grad = jnp.einsum("wihd,wjhd->whij", grad, value, preferred_element_type=jnp.float32)
        value_grad = jnp.einsum("whij,wihd->wjhd", probs, grad, preferred_element_type=jnp.float32)
        score_grad = soft * (prob_grad - jnp.sum(soft * prob_grad, axis=3, keepdims=True))
        score_grad = score_grad.astype(jnp.bfloat16)
        query_grad = jnp.einsum(
            "whij,wjhd->wihd", score_grad, key, preferred_element_type=jnp.float32
        )
        key_grad = jnp.einsum(
            "whij,wihd->wjhd", score_grad, query, preferred_element_type=jnp.float32
        )
        stacked = jnp.stack([query_grad * HEAD_DIM ** (-0.5), key_grad, value_grad], axis=3)
        stacked = stacked.astype(jnp.bfloat16).reshape(group * slots, heads * 3 * HEAD_DIM)
        return (carry + jnp.sum(score_grad.astype(jnp.float32), axis=0), stacked)

    start = jnp.zeros((heads, slots, slots), jnp.float32)
    table_grad, packed_grad = lax.scan(one, start, (tiles, grads, masks, norms))
    return (table_grad, packed_grad.reshape(windows * slots, heads * 3 * HEAD_DIM))


def on_device(
    patches,
    gain_first,
    shift_first,
    attend_weight,
    attend_bias,
    offset_table,
    output_weight,
    output_bias,
    gain_second,
    shift_second,
    expand_weight,
    expand_bias,
    reduce_weight,
    reduce_bias,
    crop_counts,
    cotangent,
):
    slots = SIDE * SIDE
    local_rows = patches.shape[0]
    local_windows = local_rows // slots
    group_live = window_live(crop_counts, crop_counts.shape[0] * 8)
    own_live = lax.dynamic_slice_in_dim(
        group_live, lax.axis_index("tensor") * local_windows, local_windows, 0
    )
    keep = own_live.reshape(local_rows, 1)
    inputs = patches.astype(jnp.float32)
    gain_one = gain_first.astype(jnp.float32)
    gain_two = gain_second.astype(jnp.float32)
    first, normal_one, scale_one = norm_rows(inputs, gain_one, shift_first.astype(jnp.float32))
    first = first.astype(jnp.bfloat16)
    w_attend, b_attend, t_offset, w_output, w_expand, b_expand, w_reduce = (
        lax.all_gather(attend_weight, "tensor", axis=1, tiled=True),
        lax.all_gather(attend_bias, "tensor", axis=0, tiled=True),
        lax.all_gather(offset_table, "tensor", axis=0, tiled=True),
        lax.all_gather(output_weight, "tensor", axis=0, tiled=True),
        lax.all_gather(expand_weight, "tensor", axis=1, tiled=True),
        lax.all_gather(expand_bias, "tensor", axis=0, tiled=True),
        lax.all_gather(reduce_weight, "tensor", axis=0, tiled=True),
    )
    heads = b_attend.shape[0]
    blank = jnp.zeros_like(b_attend[:, 0])
    bias_row = (
        jnp.stack([b_attend[:, 0], blank, b_attend[:, 1]], axis=1).reshape(-1).astype(jnp.float32)
    )
    packed = jnp.dot(first, w_attend, preferred_element_type=jnp.float32) + bias_row
    selector = offset_selector()
    relative = jnp.dot(t_offset.astype(jnp.float32), selector, precision=HIGH).reshape(
        heads, slots, slots
    )
    mixed, norms = attend_forward(packed, relative, own_live, heads)
    attended = jnp.dot(mixed, w_output, preferred_element_type=jnp.float32)
    middle = inputs + keep * (attended + output_bias.astype(jnp.float32))
    second, normal_two, scale_two = norm_rows(middle, gain_two, shift_second.astype(jnp.float32))
    second = second.astype(jnp.bfloat16)
    hidden_pre = jnp.dot(second, w_expand, preferred_element_type=jnp.float32) + b_expand.astype(
        jnp.float32
    )
    hidden = jax.nn.gelu(hidden_pre, approximate=False).astype(jnp.bfloat16)
    reduced = jnp.dot(hidden, w_reduce, preferred_element_type=jnp.float32)
    result = (middle + keep * (reduced + reduce_bias.astype(jnp.float32))).astype(jnp.bfloat16)
    upstream = cotangent.astype(jnp.float32)
    kept_up = keep * upstream
    reduce_bias_grad = jnp.sum(kept_up, axis=0)
    branch_grad = kept_up.astype(jnp.bfloat16)
    reduce_grad = tdot(hidden, branch_grad)
    hidden_grad = rdot(branch_grad, w_reduce)
    gelu_value, gelu_pull = jax.vjp(partial(jax.nn.gelu, approximate=False), hidden_pre)
    pre_grad = gelu_pull(hidden_grad)[0].astype(jnp.bfloat16)
    expand_grad = tdot(second, pre_grad)
    expand_bias_grad = jnp.sum(pre_grad.astype(jnp.float32), axis=0)
    second_grad = rdot(pre_grad, w_expand)
    middle_back, gain_two_grad, shift_two_grad = norm_back(
        second_grad, normal_two, scale_two, gain_two
    )
    middle_grad = upstream + middle_back
    kept_mid = keep * middle_grad
    output_bias_grad = jnp.sum(kept_mid, axis=0)
    attended_grad = kept_mid.astype(jnp.bfloat16)
    output_grad = tdot(mixed, attended_grad)
    mixed_grad = rdot(attended_grad, w_output).astype(jnp.bfloat16)
    relative_grad, packed_grad = attend_backward(
        packed, mixed_grad, norms, relative, own_live, heads
    )
    offset_grad = lax.dot_general(
        relative_grad.reshape(heads, slots * slots),
        selector,
        (((1,), (1,)), ((), ())),
        precision=HIGH,
    )
    attend_grad = tdot(first, packed_grad)
    packed_sum = jnp.sum(packed_grad.astype(jnp.float32), axis=0).reshape(heads, 3, HEAD_DIM)
    attend_bias_grad = jnp.stack([packed_sum[:, 0], packed_sum[:, 2]], axis=1)
    first_grad = rdot(packed_grad, w_attend)
    input_back, gain_one_grad, shift_one_grad = norm_back(
        first_grad, normal_one, scale_one, gain_one
    )
    input_grad = middle_grad + input_back
    small_grads = jnp.stack(
        [
            gain_one_grad,
            shift_one_grad,
            output_bias_grad,
            gain_two_grad,
            shift_two_grad,
            reduce_bias_grad,
        ]
    )
    (
        attend_grad,
        attend_bias_grad,
        offset_grad,
        output_grad,
        expand_grad,
        expand_bias_grad,
        reduce_grad,
        small_grads,
    ) = (
        lax.psum_scatter(
            attend_grad.astype(jnp.bfloat16), "tensor", scatter_dimension=1, tiled=True
        ).astype(jnp.float32),
        lax.psum_scatter(
            attend_bias_grad.astype(jnp.bfloat16), "tensor", scatter_dimension=0, tiled=True
        ).astype(jnp.float32),
        lax.psum_scatter(
            offset_grad.astype(jnp.bfloat16), "tensor", scatter_dimension=0, tiled=True
        ).astype(jnp.float32),
        lax.psum_scatter(
            output_grad.astype(jnp.bfloat16), "tensor", scatter_dimension=0, tiled=True
        ).astype(jnp.float32),
        lax.psum_scatter(
            expand_grad.astype(jnp.bfloat16), "tensor", scatter_dimension=1, tiled=True
        ).astype(jnp.float32),
        lax.psum_scatter(
            expand_bias_grad.astype(jnp.bfloat16), "tensor", scatter_dimension=0, tiled=True
        ).astype(jnp.float32),
        lax.psum_scatter(
            reduce_grad.astype(jnp.bfloat16), "tensor", scatter_dimension=0, tiled=True
        ).astype(jnp.float32),
        lax.psum_scatter(
            small_grads.astype(jnp.bfloat16), "tensor", scatter_dimension=1, tiled=True
        ).astype(jnp.float32),
    )
    totals = (
        lax.psum(attend_grad.astype(jnp.bfloat16), "dp").astype(jnp.float32),
        lax.psum(attend_bias_grad.astype(jnp.bfloat16), "dp").astype(jnp.float32),
        lax.psum(offset_grad.astype(jnp.bfloat16), "dp").astype(jnp.float32),
        lax.psum(output_grad.astype(jnp.bfloat16), "dp").astype(jnp.float32),
        lax.psum(expand_grad.astype(jnp.bfloat16), "dp").astype(jnp.float32),
        lax.psum(expand_bias_grad.astype(jnp.bfloat16), "dp").astype(jnp.float32),
        lax.psum(reduce_grad.astype(jnp.bfloat16), "dp").astype(jnp.float32),
        lax.psum(small_grads.astype(jnp.bfloat16), "dp").astype(jnp.float32),
    )
    smalls = totals[7]
    return (
        result,
        input_grad,
        smalls[0],
        smalls[1],
        totals[0],
        totals[1],
        totals[2],
        totals[3],
        smalls[2],
        smalls[3],
        smalls[4],
        totals[4],
        totals[5],
        totals[6],
        smalls[5],
    )


def solution(mesh):
    in_specs = (
        P(("dp", "tensor"), None),
        P(),
        P(),
        P(None, "tensor"),
        P("tensor", None, None),
        P("tensor", None),
        P("tensor", None),
        P(),
        P(),
        P(),
        P(None, "tensor"),
        P("tensor"),
        P("tensor", None),
        P(),
        P("dp"),
        P(("dp", "tensor"), None),
    )
    out_specs = (
        P(("dp", "tensor"), None),
        P(("dp", "tensor"), None),
        P("tensor"),
        P("tensor"),
        P(None, "tensor"),
        P("tensor", None, None),
        P("tensor", None),
        P("tensor", None),
        P("tensor"),
        P("tensor"),
        P("tensor"),
        P(None, "tensor"),
        P("tensor"),
        P("tensor", None),
        P("tensor"),
    )
    return jax.shard_map(
        on_device, mesh=mesh, in_specs=in_specs, out_specs=out_specs, check_vma=False
    )
```

profile of v0, /device:TPU:0, one launch (start us, length us, event | category | flops | bytes accessed | tf_op | source)
XLA Modules:
  0.0 892.9 jit_solution(10867279569873449285)
XLA Ops:
  12.0 5.3 all_gather.22
  30.2 31.6 %all-gather.7.cloned.1.call-done = bf16[768,2304]{1,0:T(8,128)(2,1)} async-done(((bf16[768,1152]{1,0:T(8,128)(2,1)}), bf16[768,2304]{1,0:T(8,128)(2,1)}) %all-gather.7.cloned.1.call-update) | async-done | bytes 3538960 | tf_op jit(solution)/shard_map/all_gather | solution.py:181
  61.8 9.5 %convolution_add_fusion = f32[1176,2304]{1,0:T(8,128)} fusion(bf16[768,2304]{1,0:T(8,128)(2,1)} %all-gather.7.cloned.1.call-done, f32[2304]{0:T(1024)S(1)} %reshape.292, bf16[1176,768]{1,0:T(8,128)(2,1)S(1)} %copy-done.4, f32[768]{0:T(1024)S(1)} %convert_element_type.189, f32[768]{0:T(1024)S(1)} %convert_element_type.188, f32[1176]{0:T(1024)S(1)} %add_rsqrt_fusion.1, ...), kind=kOutput, calls=%fused_computation.73 | convolution fusion | flops 4169926656 | bytes 16208064 | tf_op jit(solution)/shard_map/dot_general | solution.py:194
  71.3 13.2 %copy.92 = f32[1176,2304]{0,1:T(8,128)} copy(f32[1176,2304]{1,0:T(8,128)} %convolution_add_fusion) | data formatting | bytes 21676032 | tf_op jit(solution)/shard_map/add | solution.py:194
  84.5 23.0 %reshape.285 = f32[3,8,49,24,3,32]{2,1,0,5,4,3:T(8,128)} reshape(f32[1176,2304]{0,1:T(8,128)} %copy.92) | data formatting | bytes 21676032 | tf_op jit(solution)/shard_map/reshape | solution.py:96
  107.5 24.3 %copy.93 = f32[3,8,49,24,3,32]{2,5,3,1,4,0:T(8,128)} copy(f32[3,8,49,24,3,32]{2,1,0,5,4,3:T(8,128)} %reshape.285) | data formatting | bytes 21676032 | tf_op jit(solution)/shard_map/while | solution.py:113
  131.8 88.2 %while.25 = (s32[]{:T(128)}, bf16[3,392,768]{2,1,0:T(8,128)(2,1)}, f32[3,8,24,49]{3,2,1,0:T(8,128)}, f32[3,8,49,24,3,32]{2,5,3,1,4,0:T(8,128)}, f32[24,2401]{1,0...) while((s32[]{:T(128)}, bf16[3,392,768]{2,1,0:T(8,128)(2,1)}, f32[3,8,24,49]{3,2,1,0:T(8,128)}, ...), condition=%wide.region_8.9_spmd, body=%wide.region_5.8_spmd.sunk | while | flops 66335808 | bytes 27053972 | solution.py:113
  132.0 11.1 %fusion.121 = (bf16[8,49,24,3,32]{1,4,2,0,3:T(8,128)(2,1)}, f32[8,49,24,3,32]{1,4,2,0,3:T(8,128)}) fusion(f32[3,8,49,24,3,32]{2,5,3,1,4,0:T(8,128)} %get-tuple-element.399, s32[]{:T(128)} %get-tuple-element.389), kind=kLoop, calls=%fused_computation.158.clone.1 | loop fusion | flops 903168 | bytes 9031684 | tf_op jit(solution)/shard_map/convert.2
  161.1 11.9 %fusion.121 = (bf16[8,49,24,3,32]{1,4,2,0,3:T(8,128)(2,1)}, f32[8,49,24,3,32]{1,4,2,0,3:T(8,128)}) fusion(f32[3,8,49,24,3,32]{2,5,3,1,4,0:T(8,128)} %get-tuple-element.399, s32[]{:T(128)} %get-tuple-element.389), kind=kLoop, calls=%fused_computation.158.clone.1 | loop fusion | flops 903168 | bytes 9031684 | tf_op jit(solution)/shard_map/convert.2
  173.6 4.6 fusion.122
  190.9 11.2 %fusion.121 = (bf16[8,49,24,3,32]{1,4,2,0,3:T(8,128)(2,1)}, f32[8,49,24,3,32]{1,4,2,0,3:T(8,128)}) fusion(f32[3,8,49,24,3,32]{2,5,3,1,4,0:T(8,128)} %get-tuple-element.399, s32[]{:T(128)} %get-tuple-element.389), kind=kLoop, calls=%fused_computation.158.clone.1 | loop fusion | flops 903168 | bytes 9031684 | tf_op jit(solution)/shard_map/convert.2
  226.8 40.9 %multiply_convert_fusion.2 = (bf16[1176,3072]{1,0:T(8,128)(2,1)}, f32[1176,3072]{1,0:T(8,128)}, f32[1176,3072]{1,0:T(8,128)}) fusion(f32[3072]{0:T(1024)S(1)} %bitcast.161, bf16[768,3072]{1,0:T(8,128)(2,1)} %all-gather.11.cloned.1.call-done, f32[1176,768]{1,0:T(8,128)} %copy-done.6, f32[768]{0:T(1024)S(1)} %copy-done.37, f32[768]{0:T(1024)S(1)} %copy-done.25, ...), kind=kOutput, calls=%fused_computation.59 | convolution fusion | flops 5792016384 | bytes 44485824 | tf_op jit(solution)/shard_map/dot_general | solution.py:204
  267.8 19.7 %fusion.85 = (bf16[3072]{0:T(1024)(128)(2,1)}, bf16[1176,3072]{1,0:T(8,128)(2,1)}) fusion(f32[1176,3072]{1,0:T(8,128)} %get-tuple-element.254, f32[1176,3072]{1,0:T(8,128)} %get-tuple-element.269, bf16[3072,768]{1,0:T(8,128)(2,1)} %all-gather.13.cloned.1.call-done, bf16[1176,768]{1,0:T(8,128)(2,1)S(1)} %copy-done.11, f32[1176]{0:T(1024)S(1)} %copy-done.21), kind=kOutput, calls=%fused_computation.164 | convolution fusion | flops 5605960704 | bytes 42662496 | tf_op jit(solution)/shard_map/dot_general | solution.py:72
  287.5 13.2 %multiply_reduce_fusion.1 = (bf16[768]{0:T(1024)(128)(2,1)}, f32[1176]{0:T(1024)S(1)}, f32[1176]{0:T(1024)S(1)}, bf16[768]{0:T(1024)(128)(2,1)}, f32[1176,768]{1,0:T(8,128)S(1)}) fusion(f32[1176,768]{1,0:T(8,128)} %copy-done.6, f32[1176]{0:T(1024)S(1)} %add_rsqrt_fusion, f32[1176]{0:T(1024)S(1)} %broadcast_multiply_fusion.4, f32[768]{0:T(1024)S(1)} %copy-done.25, ...), kind=kOutput, calls=%fused_computation.104 | convolution fusion | flops 5557188608 | bytes 19194240 | tf_op jit(solution)/shard_map/dot_general | solution.py:72
  306.9 6.8 reshape.302
  313.7 9.2 %copy.97 = bf16[3,8,49,24,32]{2,4,3,1,0:T(8,128)(2,1)} copy(bf16[3,8,49,24,32]{4,3,2,1,0:T(8,128)(2,1)} %reshape.302) | data formatting | bytes 3612672
  322.9 159.5 %while.26 = (s32[]{:T(128)}, f32[24,49,49]{1,2,0:T(8,128)}, bf16[3,392,2304]{1,2,0:T(8,128)(2,1)}, f32[3,8,49,24,3,32]{2,5,3,1,4,0:T(8,128)}, f32[24,2401]{1,0:T...) while((s32[]{:T(128)}, f32[24,49,49]{1,2,0:T(8,128)}, ...), condition=%wide.region_16.17_spmd.clone, body=%wide.region_13.16_spmd.clone.sunk | while | flops 160520480 | bytes 91262472 | solution.py:145
  323.0 7.6 fusion.131
  330.6 6.6 fusion.132
  339.4 6.5 multiply_reduce_fusion.8
  358.7 7.6 copy.123
  366.3 6.4 convert_element_type.347
  375.3 7.6 fusion.131
  382.9 6.6 fusion.132
  391.7 6.5 multiply_reduce_fusion.8
  410.9 7.6 copy.123
  418.5 6.4 convert_element_type.347
  428.6 7.7 fusion.131
  436.3 6.6 fusion.132
  445.1 6.5 multiply_reduce_fusion.8
  464.3 7.6 copy.123
  471.9 6.4 convert_element_type.347
  482.4 9.2 %copy.98 = bf16[3,392,2304]{2,1,0:T(8,128)(2,1)} copy(bf16[3,392,2304]{1,2,0:T(8,128)(2,1)} %get-tuple-element.93) | data formatting | bytes 10838016 | tf_op jit(solution)/shard_map/while | solution.py:145
  491.6 9.2 %convolution_convert_fusion.3 = bf16[768,2304]{1,0:T(8,128)(2,1)} fusion(bf16[1176,2304]{1,0:T(8,128)(2,1)} %bitcast.156, bf16[1176,768]{1,0:T(8,128)(2,1)S(1)} %copy-done.5, f32[768]{0:T(1024)S(1)} %copy-done.40, f32[768]{0:T(1024)S(1)} %copy-done.28, f32[1176]{0:T(1024)S(1)} %copy-done.20, f32[1176]{0:T(1024)S(1)} %copy-done.16), kind=kOutput, calls=%fused_computation.80 | convolution fusion | flops 4168986624 | bytes 10779840 | tf_op jit(solution)/shard_map/dot_general | solution.py:66
  500.8 5.8 copy.108
  506.7 5.5 convolution_convert_fusion.5
  512.3 12.8 %convolution_convert_fusion.2 = bf16[768,3072]{1,0:T(8,128)(2,1)} fusion(bf16[1176,3072]{1,0:T(8,128)(2,1)} %get-tuple-element.273, f32[1176,768]{1,0:T(8,128)} %copy-done.6, f32[768]{0:T(1024)S(1)} %copy-done.38, f32[768]{0:T(1024)S(1)} %copy-done.26, f32[1176]{0:T(1024)S(1)} %copy-done.24, f32[1176]{0:T(1024)S(1)} %copy-done.18), kind=kOutput, calls=%fused_computation.79 | convolution fusion | flops 5555939328 | bytes 15572160 | tf_op jit(solution)/shard_map/dot_general | solution.py:66
  525.2 11.2 %convolution_convert_fusion.1 = bf16[3072,768]{1,0:T(8,128)(2,1)} fusion(bf16[1176,3072]{1,0:T(8,128)(2,1)} %get-tuple-element.253, bf16[1176,768]{1,0:T(8,128)(2,1)} %param.35, f32[1176]{0:T(1024)S(1)} %copy-done.22), kind=kOutput, calls=%fused_computation.78 | convolution fusion | flops 5554132992 | bytes 13754976 | tf_op jit(solution)/shard_map/dot_general | solution.py:66
  545.3 5.9 fusion
  554.6 10.6 %fusion.65 = (bf16[768]{0:T(1024)(128)(2,1)S(1)}, f32[1176]{0:T(1024)S(1)}, f32[1176]{0:T(1024)S(1)}, bf16[768]{0:T(1024)(128)(2,1)S(1)}, f32[1176,768]{1,0:T(8,128)}) fusion(bf16[1176,768]{1,0:T(8,128)(2,1)S(1)} %copy-done.5, f32[1176]{0:T(1024)S(1)} %copy-done.20, f32[1176]{0:T(1024)S(1)} %copy-done.16, f32[768]{0:T(1024)S(1)} %copy-done.28, ...), kind=kOutput, calls=%fused_computation.102 | convolution fusion | flops 4170825728 | bytes 14401920 | tf_op jit(solution)/shard_map/dot_general | solution.py:72
  566.4 7.3 all-reduce.6
  579.9 62.9 %reduce-scatter.14.cloned.1.call-done = bf16[768,1536]{1,0:T(8,128)(2,1)} async-done(((bf16[768,3072]{1,0:T(8,128)(2,1)}), bf16[768,1536]{1,0:T(8,128)(2,1)}) %reduce-scatter.14.cloned.1.call-update) | async-done | bytes 2359312 | tf_op jit(solution)/shard_map/reduce_scatter | solution.py:279
  642.8 63.0 %reduce-scatter.16.cloned.1.call-done = bf16[1536,768]{1,0:T(8,128)(2,1)} async-done(((bf16[3072,768]{1,0:T(8,128)(2,1)}), bf16[1536,768]{1,0:T(8,128)(2,1)}) %reduce-scatter.16.cloned.1.call-update) | async-done | bytes 2359312 | tf_op jit(solution)/shard_map/reduce_scatter | solution.py:285
  705.8 5.2 fusion.64
  711.0 10.5 %fusion.67 = bf16[1176,768]{1,0:T(8,128)(2,1)} fusion(f32[1176,768]{1,0:T(8,128)S(1)} %copy-done.8, bf16[1176,3072]{1,0:T(8,128)(2,1)} %get-tuple-element.253, bf16[3072,768]{1,0:T(8,128)(2,1)} %all-gather.13.cloned.1.call-done, f32[768]{0:T(1024)S(1)} %convert_element_type.199, f32[1176]{0:T(1024)S(1)} %copy-done.22), kind=kOutput, calls=%fused_computation.111 | convolution fusion | flops 5552676864 | bytes 17370720 | tf_op jit(solution)/shard_map/dot_general | solution.py:208
  722.8 64.1 %all-reduce.4 = (bf16[6,384]{1,0:T(8,128)(2,1)S(1)}, bf16[12,2,32]{2,1,0:T(2,128)(2,1)S(1)}, bf16[12,169]{1,0:T(8,128)(2,1)S(1)}, bf16[1536]{0:T(1024)(128)(2,1)S(1)}) all-reduce(bf16[6,384]{1,0:T(8,128)(2,1)S(1)} %copy.107, bf16[12,2,32]{2,1,0:T(2,128)(2,1)S(1)} %constant_dynamic-slice_fusion.1, ...), channel_id=1, replica_groups=mesh['dp'=16,'tensor'=2] {'dp'}, use_global_device_ids=true, to_apply=%region_26.27 | all-reduce | flops 6636 | bytes 26544 | tf_op jit(solution)/shard_map/psum | solution.py:300
  789.3 86.3 %all-reduce.9.cloned.1.call-done = (bf16[768,1152]{1,0:T(8,128)(2,1)}, bf16[384,768]{1,0:T(8,128)(2,1)}, bf16[768,1536]{1,0:T(8,128)(2,1)}, bf16[1536,768]{1,0:T(8,128)(2,1)}) async-done(((bf16[768,1152]{1,0:T(8,128)(2,1)}, bf16[384,768]{1,0:T(8,128)(2,1)}, bf16[768,1536]{1,0:T(8,128)(2,1)}, bf16[1536,768]{1,0:T(8,128)(2,1)}), (bf16[768,1152]{1,0:T(8,128)(2,1)}, bf16[384,768]{1,0:T(8,128)(2,1)}, ...) | async-done | bytes 7077904 | tf_op jit(solution)/shard_map/psum | solution.py:293
  875.6 4.6 convert_element_type.216
  (297 shorter events, 161.1 us)
Async XLA Ops:
  7.2 54.6 %all-gather.7.cloned.1.call-start = ((), (), s32[]{:S(2)}) async-start(), calls=%async_computation.5 | async-start | bytes 5308416 | tf_op jit(solution)/shard_map/all_gather | solution.py:181
  7.9 212.1 %all-gather.9.cloned.1.call-start = ((), (), s32[]{:S(2)}) async-start(), calls=%async_computation.6 | async-start | bytes 1769472 | tf_op jit(solution)/shard_map/all_gather | solution.py:184
  8.7 218.1 %all-gather.11.cloned.1.call-start = ((), (), s32[]{:S(2)}) async-start(), calls=%async_computation.7 | async-start | bytes 7077888 | tf_op jit(solution)/shard_map/all_gather | solution.py:185
  9.4 8.1 copy-start.44
  9.5 8.3 copy-start.34
  9.5 13.4 %copy-start.45 = (bf16[768]{0:T(1024)(128)(2,1)S(1)}, bf16[768]{0:T(1024)(128)(2,1)}, u32[]{:S(2)}) copy-start(bf16[768]{0:T(1024)(128)(2,1)} %param.27) | copy-start | bytes 4612
  9.5 14.0 %copy-start.46 = (bf16[768]{0:T(1024)(128)(2,1)S(1)}, bf16[768]{0:T(1024)(128)(2,1)}, u32[]{:S(2)}) copy-start(bf16[768]{0:T(1024)(128)(2,1)} %param.28) | copy-start | bytes 4612
  9.5 14.5 %copy-start.47 = (bf16[768]{0:T(1024)(128)(2,1)S(1)}, bf16[768]{0:T(1024)(128)(2,1)}, u32[]{:S(2)}) copy-start(bf16[768]{0:T(1024)(128)(2,1)} %param.29) | copy-start | bytes 4612
  9.5 15.1 %copy-start.42 = (bf16[1536]{0:T(1024)(128)(2,1)S(1)}, bf16[1536]{0:T(1024)(128)(2,1)}, u32[]{:S(2)}) copy-start(bf16[1536]{0:T(1024)(128)(2,1)} %param.31) | copy-start | bytes 9220
  9.5 258.2 %all-gather.13.cloned.1.call-start = ((), (), s32[]{:S(2)}) async-start(), calls=%async_computation.8 | async-start | bytes 7077888 | tf_op jit(solution)/shard_map/all_gather | solution.py:187
  10.1 563.6 %reduce-scatter.20.cloned.1.call-start = ((), (), s32[]{:S(2)}) async-start(), calls=%async_computation.13 | async-start | bytes 5308416
  11.2 60.1 %copy-start.15 = (f32[1176]{0:T(1024)}, f32[1176]{0:T(1024)S(1)}, u32[]{:S(2)}) copy-start(f32[1176]{0:T(1024)S(1)} %broadcast_multiply_fusion.5) | copy-start | bytes 14116
  11.9 59.4 %copy-start.19 = (f32[1176]{0:T(1024)}, f32[1176]{0:T(1024)S(1)}, u32[]{:S(2)}) copy-start(f32[1176]{0:T(1024)S(1)} %add_rsqrt_fusion.1) | copy-start | bytes 14116
  12.0 59.3 %copy-start.27 = (f32[768]{0:T(1024)}, f32[768]{0:T(1024)S(1)}, u32[]{:S(2)}) copy-start(f32[768]{0:T(1024)S(1)} %convert_element_type.188) | copy-start | bytes 9220
  17.5 53.8 %copy-start.39 = (f32[768]{0:T(1024)}, f32[768]{0:T(1024)S(1)}, u32[]{:S(2)}) copy-start(f32[768]{0:T(1024)S(1)} %convert_element_type.189) | copy-start | bytes 9220
  17.7 53.6 %copy-start.30 = (s32[2401]{0:T(1024)}, s32[2401]{0:T(1024)S(1)}, u32[]{:S(2)}) copy-start(s32[2401]{0:T(1024)S(1)} %reshape.296) | copy-start | bytes 28816
  131.8 88.2 %copy-start.21 = (f32[1176]{0:T(1024)S(1)}, f32[1176]{0:T(1024)}, u32[]{:S(2)}) copy-start(f32[1176]{0:T(1024)} %mul.191) | copy-start | bytes 14116
  131.8 88.2 %copy-start.41 = (f32[768]{0:T(1024)S(1)}, f32[768]{0:T(1024)}, u32[]{:S(2)}) copy-start(f32[768]{0:T(1024)} %convert_element_type.193) | copy-start | bytes 9220
  224.5 76.2 %copy-start.17 = (f32[1176]{0:T(1024)}, f32[1176]{0:T(1024)S(1)}, u32[]{:S(2)}) copy-start(f32[1176]{0:T(1024)S(1)} %broadcast_multiply_fusion.4) | copy-start | bytes 14116
  226.8 73.9 %copy-start.23 = (f32[1176]{0:T(1024)}, f32[1176]{0:T(1024)S(1)}, u32[]{:S(2)}) copy-start(f32[1176]{0:T(1024)S(1)} %add_rsqrt_fusion) | copy-start | bytes 14116
  226.8 40.9 %copy-start.11 = (bf16[1176,768]{1,0:T(8,128)(2,1)S(1)}, bf16[1176,768]{1,0:T(8,128)(2,1)}, u32[]{:S(2)}) copy-start(bf16[1176,768]{1,0:T(8,128)(2,1)} %param.35) | copy-start | bytes 5419012
  287.5 13.2 %copy-start.7 = (f32[1176,768]{1,0:T(8,128)S(1)}, f32[1176,768]{1,0:T(8,128)}, u32[]{:S(2)}) copy-start(f32[1176,768]{1,0:T(8,128)} %copy-done.6) | copy-start | bytes 10838020
  313.7 9.2 %copy-start.3 = (f32[24,2401]{1,0:T(8,128)S(1)}, f32[24,2401]{1,0:T(8,128)}, u32[]{:S(2)}) copy-start(f32[24,2401]{1,0:T(8,128)} %copy-done.2) | copy-start | bytes 691492
  330.6 6.6 copy-start
  339.4 6.5 slice-start.1
  382.9 6.6 copy-start
  391.7 6.5 slice-start
  391.7 6.5 slice-start.1
  436.3 6.6 copy-start
  445.1 6.5 slice-start
  445.1 6.5 slice-start.1
  482.4 9.2 %copy-start.5 = (bf16[1176,768]{1,0:T(8,128)(2,1)S(1)}, bf16[1176,768]{1,0:T(8,128)(2,1)}, u32[]{:S(2)}) copy-start(bf16[1176,768]{1,0:T(8,128)(2,1)} %param.20) | copy-start | bytes 5419012
  482.4 9.2 %copy-start.16 = (f32[1176]{0:T(1024)S(1)}, f32[1176]{0:T(1024)}, u32[]{:S(2)}) copy-start(f32[1176]{0:T(1024)} %copy-done.15) | copy-start | bytes 14116
  482.4 9.2 %copy-start.20 = (f32[1176]{0:T(1024)S(1)}, f32[1176]{0:T(1024)}, u32[]{:S(2)}) copy-start(f32[1176]{0:T(1024)} %copy-done.19) | copy-start | bytes 14116
  482.4 9.2 %copy-start.28 = (f32[768]{0:T(1024)S(1)}, f32[768]{0:T(1024)}, u32[]{:S(2)}) copy-start(f32[768]{0:T(1024)} %copy-done.27) | copy-start | bytes 9220
  482.4 9.2 %copy-start.40 = (f32[768]{0:T(1024)S(1)}, f32[768]{0:T(1024)}, u32[]{:S(2)}) copy-start(f32[768]{0:T(1024)} %copy-done.39) | copy-start | bytes 9220
  506.6 73.2 %reduce-scatter.12.cloned.1.call-start = ((), (), s32[]{:S(2)}) async-start(), calls=%async_computation.9 | async-start | bytes 1769472 | tf_op jit(solution)/shard_map/reduce_scatter | solution.py:276
  512.2 130.6 %reduce-scatter.14.cloned.1.call-start = ((), (), s32[]{:S(2)}) async-start(), calls=%async_computation.10 | async-start | bytes 7077888 | tf_op jit(solution)/shard_map/reduce_scatter | solution.py:279
  525.2 180.6 %reduce-scatter.16.cloned.1.call-start = ((), (), s32[]{:S(2)}) async-start(), calls=%async_computation.11 | async-start | bytes 7077888 | tf_op jit(solution)/shard_map/reduce_scatter | solution.py:285
  536.4 7.3 copy-start.1
  536.5 185.3 %reduce-scatter.18.cloned.1.call-start = ((), (), s32[]{:S(2)}) async-start(), calls=%async_computation.12 | async-start | bytes 294912
  551.2 170.4 %collective-permute-start = (bf16[4,169]{1,0:T(4,128)(2,1)S(1)}, bf16[4,169]{1,0:T(4,128)(2,1)S(1)}, u32[]{:S(2)}, u32[]{:S(2)}) collective-permute-start(bf16[4,169]{1,0:T(4,128)(2,1)S(1)} %slice.83), channel_id=1, source_target_pairs={{0,1},{2,3},{4,5},{6,7},{8,9},{10,11},{12,13},{14,15},{16,17},{18,... | collective-permute-start | bytes 4064
  554.5 10.7 %copy-start.33 = (bf16[768]{0:T(1024)(128)(2,1)S(1)}, bf16[768]{0:T(1024)(128)(2,1)}, u32[]{:S(2)}) copy-start(bf16[768]{0:T(1024)(128)(2,1)} %get-tuple-element.207) | copy-start | bytes 4612
  554.5 10.7 %copy-start.32 = (bf16[768]{0:T(1024)(128)(2,1)S(1)}, bf16[768]{0:T(1024)(128)(2,1)}, u32[]{:S(2)}) copy-start(bf16[768]{0:T(1024)(128)(2,1)} %get-tuple-element.206) | copy-start | bytes 4612
  554.5 10.7 %copy-start.50 = (bf16[768]{0:T(1024)(128)(2,1)S(1)}, bf16[768]{0:T(1024)(128)(2,1)}, u32[]{:S(2)}) copy-start(bf16[768]{0:T(1024)(128)(2,1)} %get-tuple-element.192) | copy-start | bytes 4612
  554.5 10.7 %copy-start.49 = (bf16[768]{0:T(1024)(128)(2,1)S(1)}, bf16[768]{0:T(1024)(128)(2,1)}, u32[]{:S(2)}) copy-start(bf16[768]{0:T(1024)(128)(2,1)} %get-tuple-element.198) | copy-start | bytes 4612
  554.6 11.8 %copy-start.36 = (bf16[3072]{0:T(1024)(128)(2,1)S(1)}, bf16[3072]{0:T(1024)(128)(2,1)}, u32[]{:S(2)}) copy-start(bf16[3072]{0:T(1024)(128)(2,1)} %get-tuple-element.272) | copy-start | bytes 18436
  566.3 309.3 %all-reduce.9.cloned.1.call-start = ((), (), s32[]{:S(2)}) async-start(), calls=%async_computation.14 | async-start | bytes 14155776 | tf_op jit(solution)/shard_map/psum | solution.py:293
  (25 other events, 93.8 us)
Sparse Core Ops, SparseCore 0:
  9.6 52.1 all-gather.6
  63.4 22.8 all-gather.8
  87.8 62.6 all-gather.10
  151.9 62.6 all-gather.12
  506.7 48.0 reduce-scatter.19
  557.5 22.2 reduce-scatter.11
  582.8 59.9 reduce-scatter.13
  645.8 59.9 reduce-scatter.15
  708.0 10.9 reduce-scatter.17
  723.5 152.0 all-reduce.8
where the time goes:
time: 902 us; the launch traced here: 893 us
  waiting for transfers between devices  249 us (28%)
  matrix products  243 us (27%)
  local copies, waits for them, and re-layouts  177 us (20%)
  other arithmetic  110 us (12%)
  blocking collectives  91.5 us (10%)
  between operations  17.2 us (2%)
    psum x1, waiting for transfers between devices, on_device(): lax.psum(attend_grad.astype(jnp.bfloat16), 'dp').astype(jnp.float32)  86.3 us
    psum x1, blocking collectives, on_device(): lax.psum(small_grads.astype(jnp.bfloat16), 'dp').astype(jnp.float32)  64.1 us
    reduce_scatter x1, waiting for transfers between devices, on_device(): lax.psum_scatter(reduce_grad.astype(jnp.bfloat16), 'tensor', scatter_dime...  63 us
    reduce_scatter x1, waiting for transfers between devices, on_device(): lax.psum_scatter(expand_grad.astype(jnp.bfloat16), 'tensor', scatter_dime...  62.9 us
    another operation x8, other arithmetic  57.1 us
    dot_general x4, matrix products, rdot(): lax.dot_general(left, right, (((1,), (1,)), ((), ())), preferred_element_...  45.2 us
    dot_general x1, matrix products, on_device(): jnp.dot(second, w_expand, preferred_element_type=jnp.float32)  40.9 us
    dot_general x4, matrix products, tdot(): lax.dot_general(left, right, (((0,), (0,)), ((), ())), preferred_element_...  38.7 us
  transfers between devices with their start and end apart: 11, of which 5 were waited for; matrix products, arithmetic and copies ran while one was open for 32% of the time, Pallas kernels for 0%

commit v1 on v0

--- a/solution.py
+++ b/solution.py
@@ -290,7 +290,7 @@
         ).astype(jnp.float32),
     )
     totals = (
-        lax.psum(attend_grad.astype(jnp.bfloat16), "dp").astype(jnp.float32),
+        jnp.sum(lax.all_gather(attend_grad.astype(jnp.bfloat16), "dp"), axis=0).astype(jnp.float32),
         lax.psum(attend_bias_grad.astype(jnp.bfloat16), "dp").astype(jnp.float32),
         lax.psum(offset_grad.astype(jnp.bfloat16), "dp").astype(jnp.float32),
         lax.psum(output_grad.astype(jnp.bfloat16), "dp").astype(jnp.float32),

time: 902 us -> 865 us (0.959)
  matrix products: 243 us -> 213 us
    all_gather x0 -> x1, waiting for transfers between devices: none -> 136 us  [on_device(): lax.all_gather(attend_grad.astype(jnp.bfloat16), 'dp')]
    reduce_scatter x1, waiting for transfers between devices: 63 us -> 0.02 us  [on_device(): lax.psum_scatter(reduce_grad.astype(jnp.bfloat16), 'tensor', scatter_dime...]
    reduce_scatter x1, waiting for transfers between devices: 62.9 us -> 0.02 us  [on_device(): lax.psum_scatter(expand_grad.astype(jnp.bfloat16), 'tensor', scatter_dime...]
    psum x1, waiting for transfers between devices: 86.3 us -> 36.2 us  [on_device(): lax.psum(output_grad.astype(jnp.bfloat16), 'dp').astype(jnp.float32)]
    unnamed x13 -> x14, waiting for transfers between devices: 2.7 us -> 39.3 us
    dot_general x6, matrix products: 33.6 us -> 21.1 us  [score_block(): jnp.einsum('wihd,wjhd->whij', query, key, preferred_element_type=jnp.floa...]
    reduce_sum x0 -> x1, other arithmetic: none -> 10.1 us  [on_device(): jnp.sum(lax.all_gather(attend_grad.astype(jnp.bfloat16), 'dp'), axis=0)]
    another operation x8, other arithmetic: 57.1 us -> 47.4 us
  transfers between devices with their start and end apart: 11 -> 12, of which waited for: 5 -> 4; matrix products, arithmetic and copies ran while one was open for 32% -> 53% of each run, Pallas kernels for 0% -> 0%
where the time goes in v1:
time: 865 us; the launch traced here: 856 us
  waiting for transfers between devices  244 us (28%)
  matrix products  213 us (25%)
  local copies, waits for them, and re-layouts  184 us (21%)
  other arithmetic  107 us (12%)
  blocking collectives  85.3 us (10%)
  between operations  16.8 us (2%)
    all_gather x1, waiting for transfers between devices, on_device(): lax.all_gather(attend_grad.astype(jnp.bfloat16), 'dp')  136 us
    psum x1, blocking collectives, on_device(): lax.psum(small_grads.astype(jnp.bfloat16), 'dp').astype(jnp.float32)  58.9 us
    another operation x8, other arithmetic  47.4 us
    dot_general x4, matrix products, rdot(): lax.dot_general(left, right, (((1,), (1,)), ((), ())), preferred_element_...  46.9 us
    dot_general x1, matrix products, on_device(): jnp.dot(second, w_expand, preferred_element_type=jnp.float32)  41 us
    unnamed x14, waiting for transfers between devices  39.3 us
    dot_general x4, matrix products, tdot(): lax.dot_general(left, right, (((0,), (0,)), ((), ())), preferred_element_...  36.3 us
    psum x1, waiting for transfers between devices, on_device(): lax.psum(output_grad.astype(jnp.bfloat16), 'dp').astype(jnp.float32)  36.2 us
  transfers between devices with their start and end apart: 12, of which 4 were waited for; matrix products, arithmetic and copies ran while one was open for 53% of the time, Pallas kernels for 0%

profile of v1, /device:TPU:0, one launch (start us, length us, event | category | flops | bytes accessed | tf_op | source)
XLA Modules:
  0.0 855.9 jit_solution(4179992797308479750)
XLA Ops:
  12.7 5.3 all-gather.2
  20.3 4.3 all_gather.28
  24.7 4.6 all-gather.1
  30.2 31.8 %all-gather.9.cloned.1.call-done = bf16[768,2304]{1,0:T(8,128)(2,1)} async-done(((bf16[768,1152]{1,0:T(8,128)(2,1)}), bf16[768,2304]{1,0:T(8,128)(2,1)}) %all-gather.9.cloned.1.call-update) | async-done | bytes 3538960 | tf_op jit(solution)/shard_map/all_gather | solution.py:181
  62.0 9.5 %convolution_add_fusion = f32[1176,2304]{1,0:T(8,128)} fusion(bf16[768,2304]{1,0:T(8,128)(2,1)} %all-gather.9.cloned.1.call-done, f32[2304]{0:T(1024)S(1)} %reshape.292, bf16[1176,768]{1,0:T(8,128)(2,1)S(1)} %copy-done.8, f32[768]{0:T(1024)S(1)} %convert_element_type.191, f32[768]{0:T(1024)S(1)} %convert_element_type.190, f32[1176]{0:T(1024)S(1)} %add_rsqrt_fusion.1, ...), kind=kOutput, calls=%fused_computation.73 | convolution fusion | flops 4169926656 | bytes 16208064 | tf_op jit(solution)/shard_map/dot_general | solution.py:194
  71.5 13.2 %copy.92 = f32[1176,2304]{0,1:T(8,128)} copy(f32[1176,2304]{1,0:T(8,128)} %convolution_add_fusion) | data formatting | bytes 21676032 | tf_op jit(solution)/shard_map/add | solution.py:194
  84.7 23.0 %reshape.285 = f32[3,8,49,24,3,32]{2,1,0,5,4,3:T(8,128)} reshape(f32[1176,2304]{0,1:T(8,128)} %copy.92) | data formatting | bytes 21676032 | tf_op jit(solution)/shard_map/reshape | solution.py:96
  107.7 24.3 %copy.93 = f32[3,8,49,24,3,32]{2,5,3,1,4,0:T(8,128)} copy(f32[3,8,49,24,3,32]{2,1,0,5,4,3:T(8,128)} %reshape.285) | data formatting | bytes 21676032 | tf_op jit(solution)/shard_map/while | solution.py:113
  132.0 78.2 %while.25 = (s32[]{:T(128)}, bf16[3,392,768]{2,1,0:T(8,128)(2,1)}, f32[3,8,24,49]{3,2,1,0:T(8,128)}, f32[3,8,49,24,3,32]{2,5,3,1,4,0:T(8,128)}, f32[24,2401]{1,0...) while((s32[]{:T(128)}, bf16[3,392,768]{2,1,0:T(8,128)(2,1)}, f32[3,8,24,49]{3,2,1,0:T(8,128)}, ...), condition=%wide.region_8.9_spmd, body=%wide.region_5.8_spmd.sunk | while | flops 66335808 | bytes 28435136 | solution.py:113
  133.6 7.6 fusion.121
  147.1 4.3 fusion.124
  159.3 8.6 %fusion.121 = (bf16[8,49,24,3,32]{1,4,2,0,3:T(8,128)(2,1)}, f32[8,49,24,3,32]{1,4,2,0,3:T(8,128)S(1)}) fusion(f32[3,8,49,24,3,32]{2,5,3,1,4,0:T(8,128)} %get-tuple-element.398, s32[]{:T(128)S(6)} %copy.131), kind=kLoop, calls=%fused_computation.158.clone.1 | loop fusion | flops 903168 | bytes 9031684 | tf_op jit(solution)/shard_map/convert.3
  173.7 4.3 fusion.124
  185.9 7.7 fusion.121
  199.4 4.3 fusion.124
  210.2 4.3 fusion.84
  217.0 41.0 %multiply_convert_fusion.2 = (bf16[1176,3072]{1,0:T(8,128)(2,1)}, f32[1176,3072]{1,0:T(8,128)}, f32[1176,3072]{1,0:T(8,128)}) fusion(f32[3072]{0:T(1024)S(1)} %bitcast.161, bf16[768,3072]{1,0:T(8,128)(2,1)} %all-gather.13.cloned.1.call-done, f32[1176,768]{1,0:T(8,128)} %copy-done.10, f32[768]{0:T(1024)S(1)} %copy-done.36, f32[768]{0:T(1024)S(1)} %copy-done.23, ...), kind=kOutput, calls=%fused_computation.59 | convolution fusion | flops 5792016384 | bytes 44485824 | tf_op jit(solution)/shard_map/dot_general | solution.py:204
  258.0 19.4 %fusion.85 = (bf16[3072]{0:T(1024)(128)(2,1)}, bf16[1176,3072]{1,0:T(8,128)(2,1)}) fusion(f32[1176,3072]{1,0:T(8,128)} %get-tuple-element.253, f32[1176,3072]{1,0:T(8,128)} %get-tuple-element.268, bf16[3072,768]{1,0:T(8,128)(2,1)} %all-gather.15.cloned.1.call-done, bf16[1176,768]{1,0:T(8,128)(2,1)S(1)} %copy-done.15, f32[1176]{0:T(1024)S(1)} %copy-done.19), kind=kOutput, calls=%fused_computation.164 | convolution fusion | flops 5605960704 | bytes 42662496 | tf_op jit(solution)/shard_map/dot_general | solution.py:72
  277.5 13.2 %multiply_reduce_fusion.1 = (bf16[768]{0:T(1024)(128)(2,1)}, f32[1176]{0:T(1024)S(1)}, f32[1176]{0:T(1024)S(1)}, bf16[768]{0:T(1024)(128)(2,1)}, f32[1176,768]{1,0:T(8,128)S(1)}) fusion(f32[1176,768]{1,0:T(8,128)} %copy-done.10, f32[1176]{0:T(1024)S(1)} %add_rsqrt_fusion, f32[1176]{0:T(1024)S(1)} %broadcast_multiply_fusion.4, f32[768]{0:T(1024)S(1)} %copy-done.23, ...), kind=kOutput, calls=%fused_computation.104 | convolution fusion | flops 5557188608 | bytes 19194240 | tf_op jit(solution)/shard_map/dot_general | solution.py:72
  298.3 12.1 %convolution_convert_fusion.1 = bf16[3072,768]{1,0:T(8,128)(2,1)} fusion(bf16[1176,3072]{1,0:T(8,128)(2,1)} %get-tuple-element.252, bf16[1176,768]{1,0:T(8,128)(2,1)S(1)} %copy-done.15, f32[1176]{0:T(1024)S(1)} %copy-done.19), kind=kOutput, calls=%fused_computation.78 | convolution fusion | flops 5554132992 | bytes 13754976 | tf_op jit(solution)/shard_map/dot_general | solution.py:66
  315.4 6.8 reshape.303
  322.2 9.3 %copy.97 = bf16[3,8,49,24,32]{2,4,3,1,0:T(8,128)(2,1)} copy(bf16[3,8,49,24,32]{4,3,2,1,0:T(8,128)(2,1)} %reshape.303) | data formatting | bytes 3612672
  331.5 11.9 %convolution_convert_fusion.2 = bf16[768,3072]{1,0:T(8,128)(2,1)} fusion(bf16[1176,3072]{1,0:T(8,128)(2,1)} %get-tuple-element.272, f32[1176,768]{1,0:T(8,128)} %copy-done.10, f32[768]{0:T(1024)S(1)} %copy-done.36, f32[768]{0:T(1024)S(1)} %copy-done.23, f32[1176]{0:T(1024)S(1)} %add_rsqrt_fusion, f32[1176]{0:T(1024)S(1)} %broadcast_multiply_fusion.4), kind=kOutput, calls=%fused_computation.79 | convolution fusion | flops 5555939328 | bytes 15572160 | tf_op jit(solution)/shard_map/dot_general | solution.py:66
  344.4 130.9 %while.26 = (s32[]{:T(128)}, f32[24,49,49]{1,2,0:T(8,128)}, bf16[3,392,2304]{1,2,0:T(8,128)(2,1)}, f32[3,8,49,24,3,32]{2,5,3,1,4,0:T(8,128)}, f32[24,2401]{1,0:T...) while((s32[]{:T(128)}, f32[24,49,49]{1,2,0:T(8,128)}, ...), condition=%wide.region_16.17_spmd.clone, body=%wide.region_13.16_spmd.clone.sunk | while | flops 160520480 | bytes 74468408 | solution.py:145
  347.8 7.6 fusion.131
  372.4 7.7 copy.124
  380.1 6.4 convert_element_type.349
  391.2 8.1 fusion.131
  416.2 7.7 copy.124
  423.9 6.4 convert_element_type.349
  434.9 7.7 fusion.131
  459.5 7.7 copy.124
  467.1 6.4 convert_element_type.349
  475.4 9.1 %copy.98 = bf16[3,392,2304]{2,1,0:T(8,128)(2,1)} copy(bf16[3,392,2304]{1,2,0:T(8,128)(2,1)} %get-tuple-element.93) | data formatting | bytes 10838016 | tf_op jit(solution)/shard_map/while | solution.py:145
  484.5 9.2 %convolution_convert_fusion.3 = bf16[768,2304]{1,0:T(8,128)(2,1)} fusion(bf16[1176,2304]{1,0:T(8,128)(2,1)} %bitcast.156, bf16[1176,768]{1,0:T(8,128)(2,1)S(1)} %copy-done.9, f32[768]{0:T(1024)S(1)} %copy-done.35, f32[768]{0:T(1024)S(1)} %copy-done.25, f32[1176]{0:T(1024)S(1)} %copy-done.22, f32[1176]{0:T(1024)S(1)} %copy-done.18), kind=kOutput, calls=%fused_computation.80 | convolution fusion | flops 4168986624 | bytes 10779840 | tf_op jit(solution)/shard_map/dot_general | solution.py:66
  493.7 5.8 copy.108
  499.7 10.6 %fusion.65 = (bf16[768]{0:T(1024)(128)(2,1)S(1)}, f32[1176]{0:T(1024)S(1)}, f32[1176]{0:T(1024)S(1)}, bf16[768]{0:T(1024)(128)(2,1)S(1)}, f32[1176,768]{1,0:T(8,128)}) fusion(bf16[1176,768]{1,0:T(8,128)(2,1)S(1)} %copy-done.9, f32[1176]{0:T(1024)S(1)} %copy-done.22, f32[1176]{0:T(1024)S(1)} %copy-done.18, f32[768]{0:T(1024)S(1)} %copy-done.25, ...), kind=kOutput, calls=%fused_computation.102 | convolution fusion | flops 4170825728 | bytes 14401920 | tf_op jit(solution)/shard_map/dot_general | solution.py:72
  511.9 36.1 %reduce-scatter.20.cloned.1.call-done = bf16[1152,768]{1,0:T(8,128)(2,1)} async-done(((bf16[2304,768]{1,0:T(8,128)(2,1)}), bf16[1152,768]{1,0:T(8,128)(2,1)}) %reduce-scatter.20.cloned.1.call-update) | async-done | bytes 1769488
  554.5 4.2 reduce.3
  560.2 5.3 fusion
  569.3 6.9 all-reduce.6
  576.3 5.5 fusion.64
  581.8 10.5 %fusion.67 = bf16[1176,768]{1,0:T(8,128)(2,1)} fusion(f32[1176,768]{1,0:T(8,128)S(1)} %copy-done.12, bf16[1176,3072]{1,0:T(8,128)(2,1)} %get-tuple-element.252, bf16[3072,768]{1,0:T(8,128)(2,1)} %all-gather.15.cloned.1.call-done, f32[768]{0:T(1024)S(1)} %convert_element_type.201, f32[1176]{0:T(1024)S(1)} %copy-done.20), kind=kOutput, calls=%fused_computation.111 | convolution fusion | flops 5552676864 | bytes 17370720 | tf_op jit(solution)/shard_map/dot_general | solution.py:208
  593.6 58.9 %all-reduce.4 = (bf16[6,384]{1,0:T(8,128)(2,1)S(1)}, bf16[12,2,32]{2,1,0:T(2,128)(2,1)S(1)}, bf16[12,169]{1,0:T(8,128)(2,1)S(1)}, bf16[1536]{0:T(1024)(128)(2,1)S(1)}) all-reduce(bf16[6,384]{1,0:T(8,128)(2,1)S(1)} %copy.107, bf16[12,2,32]{2,1,0:T(2,128)(2,1)S(1)} %constant_dynamic-slice_fusion.1, ...), channel_id=1, replica_groups=mesh['dp'=16,'tensor'=2] {'dp'}, use_global_device_ids=true, to_apply=%region_26.27 | all-reduce | flops 6636 | bytes 26544 | tf_op jit(solution)/shard_map/psum | solution.py:300
  655.0 36.2 %all-reduce.9.cloned.1.call-done = (bf16[384,768]{1,0:T(8,128)(2,1)}, bf16[768,1536]{1,0:T(8,128)(2,1)}, bf16[1536,768]{1,0:T(8,128)(2,1)}) async-done(((bf16[384,768]{1,0:T(8,128)(2,1)}, bf16[768,1536]{1,0:T(8,128)(2,1)}, bf16[1536,768]{1,0:T(8,128)(2,1)}), (bf16[384,768]{1,0:T(8,128)(2,1)}, bf16[768,1536]{1,0:T(8,128)(2,1)}, bf16[1536,768]{1,0:T(8,128)(2,1)})) %all-reduce.9.cloned.1.call-update) | async-done | bytes 5308432 | tf_op jit(solution)/shard_map/psum | solution.py:296
  693.4 4.6 convert_element_type.218
  700.7 136.3 %all-gather.17.cloned.1.call-done = bf16[12288,1152]{1,0:T(8,128)(2,1)} async-done(((bf16[768,1152]{1,0:T(8,128)(2,1)}), bf16[12288,1152]{1,0:T(8,128)(2,1)}) %all-gather.17.cloned.1.call-update) | async-done | bytes 28311568 | tf_op jit(solution)/shard_map/all_gather | solution.py:293
  837.0 10.1 %reduce_sum.210 = bf16[768,1152]{1,0:T(8,128)(2,1)S(1)} reduce(bf16[16,768,1152]{2,1,0:T(8,128)(2,1)} %bitcast.154, bf16[]{:T(256)} %constant.57.clone.1), dimensions={0}, to_apply=%region_28.29 | reduce | flops 13271040 | bytes 30081026 | tf_op jit(solution)/shard_map/reduce_sum | solution.py:293
  (296 shorter events, 151.9 us)
Async XLA Ops:
  7.2 4.3 copy-start.41
  7.2 4.3 copy-start.42
  7.2 4.9 copy-start.43
  7.2 5.5 copy-start.38
  7.3 11.3 %copy-start.8 = (bf16[1176,768]{1,0:T(8,128)(2,1)S(1)}, bf16[1176,768]{1,0:T(8,128)(2,1)}, u32[]{:S(2)}) copy-start(bf16[1176,768]{1,0:T(8,128)(2,1)} %param.20) | copy-start | bytes 5419012
  7.3 54.7 %all-gather.9.cloned.1.call-start = ((), (), s32[]{:S(2)}) async-start(), calls=%async_computation.5 | async-start | bytes 5308416 | tf_op jit(solution)/shard_map/all_gather | solution.py:181
  8.0 202.2 %all-gather.11.cloned.1.call-start = ((), (), s32[]{:S(2)}) async-start(), calls=%async_computation.6 | async-start | bytes 1769472 | tf_op jit(solution)/shard_map/all_gather | solution.py:184
  8.7 208.2 %all-gather.13.cloned.1.call-start = ((), (), s32[]{:S(2)}) async-start(), calls=%async_computation.7 | async-start | bytes 7077888 | tf_op jit(solution)/shard_map/all_gather | solution.py:185
  9.5 10.8 %copy-start.32 = (bf16[12,2,32]{2,1,0:T(2,128)(2,1)S(1)}, bf16[12,2,32]{2,1,0:T(2,128)(2,1)}, u32[]{:S(2)}) copy-start(bf16[12,2,32]{2,1,0:T(2,128)(2,1)} %param.24) | copy-start | bytes 4612
  9.5 15.2 %copy-start.31 = (bf16[12,169]{1,0:T(8,128)(2,1)S(1)}, bf16[12,169]{1,0:T(8,128)(2,1)}, u32[]{:S(2)}) copy-start(bf16[12,169]{1,0:T(8,128)(2,1)} %param.25) | copy-start | bytes 12172
  9.5 248.5 %all-gather.15.cloned.1.call-start = ((), (), s32[]{:S(2)}) async-start(), calls=%async_computation.8 | async-start | bytes 7077888 | tf_op jit(solution)/shard_map/all_gather | solution.py:187
  10.1 501.2 %reduce-scatter.12.cloned.1.call-start = ((), (), s32[]{:S(2)}) async-start(), calls=%async_computation.9 | async-start | bytes 1769472 | tf_op jit(solution)/shard_map/reduce_scatter | solution.py:276
  10.9 60.5 %copy-start.24 = (f32[768]{0:T(1024)}, f32[768]{0:T(1024)S(1)}, u32[]{:S(2)}) copy-start(f32[768]{0:T(1024)S(1)} %convert_element_type.190) | copy-start | bytes 9220
  11.5 59.9 %copy-start.34 = (f32[768]{0:T(1024)}, f32[768]{0:T(1024)S(1)}, u32[]{:S(2)}) copy-start(f32[768]{0:T(1024)S(1)} %convert_element_type.191) | copy-start | bytes 9220
  18.9 52.5 %copy-start.17 = (f32[1176]{0:T(1024)}, f32[1176]{0:T(1024)S(1)}, u32[]{:S(2)}) copy-start(f32[1176]{0:T(1024)S(1)} %broadcast_multiply_fusion.5) | copy-start | bytes 14116
  19.6 51.8 %copy-start.21 = (f32[1176]{0:T(1024)}, f32[1176]{0:T(1024)S(1)}, u32[]{:S(2)}) copy-start(f32[1176]{0:T(1024)S(1)} %add_rsqrt_fusion.1) | copy-start | bytes 14116
  29.8 41.7 %copy-start.27 = (s32[2401]{0:T(1024)}, s32[2401]{0:T(1024)S(1)}, u32[]{:S(2)}) copy-start(s32[2401]{0:T(1024)S(1)} %reshape.296) | copy-start | bytes 28816
  132.0 78.2 %copy-start.19 = (f32[1176]{0:T(1024)S(1)}, f32[1176]{0:T(1024)}, u32[]{:S(2)}) copy-start(f32[1176]{0:T(1024)} %mul.191) | copy-start | bytes 14116
  132.0 78.2 %copy-start.37 = (f32[768]{0:T(1024)S(1)}, f32[768]{0:T(1024)}, u32[]{:S(2)}) copy-start(f32[768]{0:T(1024)} %convert_element_type.195) | copy-start | bytes 9220
  210.1 4.4 copy-start.6
  210.2 4.4 copy-start.16
  217.0 41.1 %copy-start.15 = (bf16[1176,768]{1,0:T(8,128)(2,1)S(1)}, bf16[1176,768]{1,0:T(8,128)(2,1)}, u32[]{:S(2)}) copy-start(bf16[1176,768]{1,0:T(8,128)(2,1)} %param.35) | copy-start | bytes 5419012
  277.5 13.2 %copy-start.11 = (f32[1176,768]{1,0:T(8,128)S(1)}, f32[1176,768]{1,0:T(8,128)}, u32[]{:S(2)}) copy-start(f32[1176,768]{1,0:T(8,128)} %copy-done.10) | copy-start | bytes 10838020
  290.7 4.5 copy-start.48
  298.3 213.0 %reduce-scatter.16.cloned.1.call-start = ((), (), s32[]{:S(2)}) async-start(), calls=%async_computation.11 | async-start | bytes 7077888 | tf_op jit(solution)/shard_map/reduce_scatter | solution.py:285
  310.5 200.8 %reduce-scatter.14.cloned.1.call-start = ((), (), s32[]{:S(2)}) async-start(), calls=%async_computation.10 | async-start | bytes 7077888 | tf_op jit(solution)/shard_map/reduce_scatter | solution.py:279
  343.5 204.5 %reduce-scatter.20.cloned.1.call-start = ((), (), s32[]{:S(2)}) async-start(), calls=%async_computation.14 | async-start | bytes 5308416
  475.3 9.2 %copy-start.9 = (bf16[1176,768]{1,0:T(8,128)(2,1)S(1)}, bf16[1176,768]{1,0:T(8,128)(2,1)}, u32[]{:S(2)}) copy-start(bf16[1176,768]{1,0:T(8,128)(2,1)} %param.20) | copy-start | bytes 5419012
  475.3 9.2 %copy-start.18 = (f32[1176]{0:T(1024)S(1)}, f32[1176]{0:T(1024)}, u32[]{:S(2)}) copy-start(f32[1176]{0:T(1024)} %copy-done.17) | copy-start | bytes 14116
  475.3 9.2 %copy-start.22 = (f32[1176]{0:T(1024)S(1)}, f32[1176]{0:T(1024)}, u32[]{:S(2)}) copy-start(f32[1176]{0:T(1024)} %copy-done.21) | copy-start | bytes 14116
  475.3 9.2 %copy-start.25 = (f32[768]{0:T(1024)S(1)}, f32[768]{0:T(1024)}, u32[]{:S(2)}) copy-start(f32[768]{0:T(1024)} %copy-done.24) | copy-start | bytes 9220
  475.4 9.2 %copy-start.35 = (f32[768]{0:T(1024)S(1)}, f32[768]{0:T(1024)}, u32[]{:S(2)}) copy-start(f32[768]{0:T(1024)} %copy-done.34) | copy-start | bytes 9220
  493.7 5.9 copy-start.46
  493.7 5.9 copy-start.45
  493.7 5.9 copy-start.30
  493.7 6.0 copy-start.29
  499.5 93.1 %reduce-scatter.18.cloned.1.call-start = ((), (), s32[]{:S(2)}) async-start(), calls=%async_computation.13 | async-start | bytes 294912
  511.2 180.0 %all-reduce.9.cloned.1.call-start = ((), (), s32[]{:S(2)}) async-start(), calls=%async_computation.15 | async-start | bytes 10616832 | tf_op jit(solution)/shard_map/psum | solution.py:296
  511.8 40.1 %copy-start.47 = (u32[32]{0:T(128)S(1)}, u32[32]{0:T(128)}, u32[]{:S(2)}) copy-start(u32[32]{0:T(128)} %constant.183) | copy-start | bytes 388
  511.8 42.6 %copy-start.44 = (bf16[768]{0:T(1024)(128)(2,1)S(1)}, bf16[768]{0:T(1024)(128)(2,1)}, u32[]{:S(2)}) copy-start(bf16[768]{0:T(1024)(128)(2,1)} %param.33) | copy-start | bytes 4612
  511.8 325.2 %all-gather.17.cloned.1.call-start = ((), (), s32[]{:S(2)}) async-start(), calls=%async_computation.12 | async-start | bytes 30081024 | tf_op jit(solution)/shard_map/all_gather | solution.py:293
  551.8 6.8 copy-start.5
  554.4 4.8 copy-start.28
  554.4 14.9 %copy-start.33 = (bf16[3072]{0:T(1024)(128)(2,1)S(1)}, bf16[3072]{0:T(1024)(128)(2,1)}, u32[]{:S(2)}) copy-start(bf16[3072]{0:T(1024)(128)(2,1)} %get-tuple-element.271) | copy-start | bytes 18436
  565.5 27.0 %collective-permute-start = (bf16[4,169]{1,0:T(4,128)(2,1)S(1)}, bf16[4,169]{1,0:T(4,128)(2,1)S(1)}, u32[]{:S(2)}, u32[]{:S(2)}) collective-permute-start(bf16[4,169]{1,0:T(4,128)(2,1)S(1)} %slice.83), channel_id=1, source_target_pairs={{0,1},{2,3},{4,5},{6,7},{8,9},{10,11},{12,13},{14,15},{16,17},{18,... | collective-permute-start | bytes 4064
  576.3 5.6 copy-start.12
  576.3 5.6 copy-start.20
  693.4 4.7 copy-start.14
  (25 other events, 61.3 us)
Sparse Core Ops, SparseCore 0:
  9.6 52.2 all-gather.8
  63.5 22.8 all-gather.10
  87.9 62.6 all-gather.12
  152.0 62.6 all-gather.14
  298.4 22.0 reduce-scatter.11
  322.7 59.9 reduce-scatter.15
  385.6 59.9 reduce-scatter.13
  499.6 48.2 reduce-scatter.19
  550.2 10.9 reduce-scatter.17
  565.1 126.0 all-reduce.8
  693.5 143.4 all-gather.16
